TPU v7x, 32 devices: a whole 2x2x4 slice. The times are simulated.
32 devices in a mesh: row: 2 (over y), col: 16 (over z, x, core).
Axes of the slice: x: 2, y: 2, z: 4, core: 2. Of those that a mesh axis runs over, the one named last changes fastest.
Arguments:
- active_matrix: float32 [16384, 16384], P('row', 'col'), may hold values from -6 to 6
- schur_rows: float32 [512, 16384], P('row', 'col'), may hold values from -6 to 6
- accum_first: float32 [32, 512, 512], P('row', 'col'), may hold values from -1 to 1, as said below
- accum_second: float32 [32, 512, 512], P('row', 'col'), may hold values from -1 to 1, as said below
Outputs:
- matrix_out: float32 [16384, 16384], P('row', 'col')
- schur_out: float32 [512, 16384], P('row', 'col')
Inputs may be any that keep to these rules, and one draw needn't show every extreme that they name: `accum_first`: each of the 32 blocks of order 512 is an orthogonal matrix. `accum_second`: each of the 32 blocks of order 512 is an orthogonal matrix.
All inputs are finite; a program needn't handle non-finite values.
Results may differ from a plain program's by a relative error of at most 0.000098.
Values sent between devices are 32-bit elements; how exact they have to be, the bound alone decides.
No kernel may reach another device: no remote copies, remote signals or barrier semaphores. Data moves between devices by JAX's collectives and lax.ppermute only.
A program may use at most 256 MiB of HBM per device.

v0:
```python
import jax
import jax.numpy as jnp
from jax import lax
from jax.sharding import PartitionSpec as P


def spread(array, axis, root):
    mine = lax.axis_index(axis) == root
    return lax.psum(jnp.where(mine, array, jnp.zeros_like(array)), axis)


def passed_along(block, axis, distance):
    devices = range(lax.axis_size(axis))
    route = [((i - distance) % len(devices), i) for i in devices]
    return lax.ppermute(block, axis, route)


def padded(block, sides, width):
    for axis, dim in sides:
        count = lax.axis_size(axis)
        forward = [(i, i + 1) for i in range(count - 1)]
        forward.append((count - 1, 0))
        backward = [(target, source) for source, target in forward]
        low = lax.ppermute(
            lax.slice_in_dim(block, block.shape[dim] - width, None, axis=dim), axis, forward
        )
        high = lax.ppermute(lax.slice_in_dim(block, 0, width, axis=dim), axis, backward)
        block = jnp.concatenate([low, block, high], axis=dim)
    return block


def exact_dot(left, right):
    return jnp.dot(left, right, precision=lax.Precision.HIGHEST, preferred_element_type=jnp.float32)


def aligned_right(matrix, blocks):
    rows, cols = matrix.shape
    count, width = (blocks.shape[0], blocks.shape[1])
    shaped = matrix.reshape(rows, count, width)
    out = jnp.einsum("nki,kij->nkj", shaped, blocks, precision=lax.Precision.HIGHEST)
    return out.reshape(rows, cols)


def straddle_right(extended, blocks, half):
    rows = extended.shape[0]
    width = blocks.shape[1]
    count = blocks.shape[0] - 1
    head = exact_dot(extended[:, :width], blocks[0][:, half:])
    tail = exact_dot(extended[:, count * width :], blocks[count][:, :half])
    pieces = [head]
    if count > 1:
        inner = extended[:, width : count * width].reshape(rows, count - 1, width)
        middle = jnp.einsum("nki,kij->nkj", inner, blocks[1:count], precision=lax.Precision.HIGHEST)
        pieces.append(middle.reshape(rows, (count - 1) * width))
    pieces.append(tail)
    return jnp.concatenate(pieces, axis=1)


def straddle_left(blocks, extended, half):
    cols = extended.shape[1]
    width = blocks.shape[1]
    count = blocks.shape[0] - 1
    head = jnp.einsum(
        "ij,in->jn", blocks[0][:, half:], extended[:width], precision=lax.Precision.HIGHEST
    )
    tail = jnp.einsum(
        "ij,in->jn",
        blocks[count][:, :half],
        extended[count * width :],
        precision=lax.Precision.HIGHEST,
    )
    pieces = [head]
    inner = extended[width : count * width].reshape(count - 1, width, cols)
    middle = jnp.einsum("kij,kin->kjn", blocks[1:count], inner, precision=lax.Precision.HIGHEST)
    pieces.append(middle.reshape((count - 1) * width, cols))
    pieces.append(tail)
    return jnp.concatenate(pieces, axis=0)


def per_device(active_matrix, schur_rows, accum_first, accum_second):
    width = accum_first.shape[2]
    half = width // 2
    row_tile, col_tile = active_matrix.shape
    per_row = row_tile // width
    per_col = col_tile // width
    col_index = lax.axis_index("col")
    owner_row = col_index * per_col // per_row
    owner_offset = col_index * per_col % per_row
    first_full = lax.all_gather(accum_first, "col", axis=1, tiled=True)
    shaped = active_matrix.reshape(per_row, width, col_tile)
    turned_rows = jnp.einsum(
        "kij,kin->kjn", first_full, shaped, precision=lax.Precision.HIGHEST
    ).reshape(row_tile, col_tile)
    chosen = lax.dynamic_slice_in_dim(first_full, owner_offset, per_col, 0)
    first_cols = spread(chosen, "row", owner_row)
    stacked = jnp.concatenate([turned_rows, schur_rows], axis=0)
    turned = aligned_right(stacked, first_cols)
    second_full = lax.all_gather(accum_second, "col", axis=1, tiled=True)
    chosen_second = lax.dynamic_slice_in_dim(second_full, owner_offset, per_col, 0)
    second_cols = spread(chosen_second, "row", owner_row)
    next_col = passed_along(second_cols[0:1], "col", -1)
    col_blocks = jnp.concatenate([second_cols, next_col], axis=0)
    next_row = passed_along(second_full[0:1], "row", -1)
    row_blocks = jnp.concatenate([second_full, next_row], axis=0)
    extended = padded(turned, (("col", 1),), half)
    moved = straddle_right(extended, col_blocks, half)
    matrix_part = moved[:row_tile]
    schur_out = moved[row_tile:]
    extended_rows = padded(matrix_part, (("row", 0),), half)
    matrix_out = straddle_left(row_blocks, extended_rows, half)
    return (matrix_out, schur_out)


def solution(mesh):
    in_specs = (P("row", "col"), P("row", "col"), P("row", "col", None), P("row", "col", None))
    out_specs = (P("row", "col"), P("row", "col"))
    return jax.shard_map(
        per_device, mesh=mesh, in_specs=in_specs, out_specs=out_specs, check_vma=False
    )
```

profile of v0, /device:TPU:1, one launch (start us, length us, event | category | flops | bytes accessed | tf_op | source)
XLA Modules:
  0.0 975.9 jit_solution(12555701314665027359)
XLA Ops:
  8.7 130.4 %all-gather.3.cloned.1.call-done = f32[16,512,512]{2,1,0:T(8,128)} async-done(((f32[16,32,512]{2,1,0:T(8,128)}), f32[16,512,512]{2,1,0:T(8,128)}) %all-gather.3.cloned.1.call-update) | async-done | bytes 16777232 | tf_op jit(solution)/shard_map/all_gather | solution.py:89
  139.1 3.2 dynamic-slice_select_fusion.1
  142.3 123.7 %all-gather.5.cloned.1.call-done = f32[16,512,512]{2,1,0:T(8,128)} async-done(((f32[16,32,512]{2,1,0:T(8,128)}), f32[16,512,512]{2,1,0:T(8,128)}) %all-gather.5.cloned.1.call-update) | async-done | bytes 16777232 | tf_op jit(solution)/shard_map/all_gather | solution.py:98
  266.0 3.1 dynamic-slice_select_fusion
  271.0 60.6 %fusion.31 = f32[16,512,1024]{2,1,0:T(8,128)} fusion(f32[16,512,512]{2,1,0:T(8,128)} %all-gather.3.cloned.1.call-done, f32[16,512,1024]{2,1,0:T(8,128)} %bitcast.40), kind=kOutput, calls=%fused_computation.43 | convolution fusion | flops 51539607552 | bytes 83886080 | tf_op jit(solution)/shard_map/kij,kin->kjn/dot_general | solution.py:91
  331.6 42.7 %concatenate.28 = f32[8192,2,512]{2,1,0:T(2,128)} reshape(f32[16,512,1024]{2,1,0:T(8,128)} %fusion.31) | data formatting | bytes 67108864 | tf_op jit(solution)/shard_map/concatenate | solution.py:96
  374.3 27.6 %copy.12 = f32[8192,2,512]{2,0,1:T(8,128)} copy(f32[8192,2,512]{2,1,0:T(2,128)} %concatenate.28) | data formatting | bytes 67108864 | tf_op jit(solution)/shard_map/concatenate | solution.py:96
  401.9 115.2 %fusion = f32[2,512,8448]{2,1,0:T(8,128)} fusion(f32[2,512,512]{2,1,0:T(8,128)} %get-tuple-element.6, f32[256,2,512]{2,0,1:T(8,128)S(1)} %copy.13, f32[8192,2,512]{2,0,1:T(8,128)} %copy.12), kind=kOutput, calls=%fused_computation | convolution fusion | flops 53158871040 | bytes 71303168 | tf_op jit(solution)/shard_map/nki,kij->nkj/dot_general | solution.py:40
  517.1 12.2 %fusion.30 = (f32[8448,256]{0,1:T(8,128)}, f32[8448,256]{0,1:T(8,128)}) fusion(f32[8448,1024]{0,1:T(8,128)} %bitcast.34), kind=kLoop, calls=%fused_computation.42 | loop fusion | bytes 34603008 | tf_op jit(solution)/shard_map/slice | solution.py:25
  531.0 2.9 slice_bitcast_fusion.2
  535.4 34.6 %fusion.12 = f32[8448,512]{0,1:T(8,128)S(1)} fusion(f32[8448,1024]{0,1:T(8,128)} %bitcast.35, f32[2,512,512]{2,1,0:T(8,128)S(1)} %copy-done.2), kind=kOutput, calls=%fused_computation.16 | convolution fusion | flops 26575110144 | bytes 35651584 | tf_op jit(solution)/shard_map/nki,kij->nkj/dot_general | solution.py:53
  570.0 159.1 %collective-permute-done.2 = f32[1,512,512]{2,1,0:T(8,128)S(1)} collective-permute-done((f32[1,512,512]{2,1,0:T(8,128)S(1)}, f32[1,512,512]{2,1,0:T(8,128)S(1)}, u32[]{:S(2)}, u32[]{:S(2)}) %collective-permute-start.2) | collective-permute-done | bytes 1048608 | tf_op jit(solution)/shard_map/ppermute | solution.py:15
  730.1 20.4 %fusion.4 = f32[8448,256]{0,1:T(8,128)} fusion(f32[8448,256]{0,1:T(8,128)} %collective-permute-done.1, f32[8448,1024]{0,1:T(8,128)} %bitcast.36, f32[512,512]{1,0:T(8,128)} %bitcast.42), kind=kOutput, calls=%fused_computation.7 | convolution fusion | flops 13291880448 | bytes 52428800 | tf_op jit(solution)/shard_map/dot_general | solution.py:33
  750.5 20.5 %fusion.8 = f32[8448,256]{0,1:T(8,128)} fusion(f32[8448,1024]{0,1:T(8,128)} %bitcast.37, f32[8448,256]{0,1:T(8,128)} %collective-permute-done, f32[512,512]{1,0:T(8,128)S(1)} %get-tuple-element.15), kind=kOutput, calls=%fused_computation.12 | convolution fusion | flops 13291880448 | bytes 52428800 | tf_op jit(solution)/shard_map/dot_general | solution.py:33
  771.1 1.6 pad_maximum_fusion.14
  772.7 23.2 %pad_maximum_fusion = f32[8448,1024]{0,1:T(8,128)} fusion(f32[8448,256]{0,1:T(8,128)} %fusion.4, f32[8448,512]{0,1:T(8,128)} %copy-done.1, f32[8448,256]{0,1:T(8,128)} %fusion.8), kind=kLoop, calls=%fused_computation.4 | loop fusion | flops 17301504 | bytes 69206016 | tf_op jit(solution)/shard_map/concatenate | solution.py:56
  797.1 21.7 %slice.99 = f32[7680,1024]{0,1:T(8,128)} slice(f32[8448,1024]{0,1:T(8,128)} %pad_maximum_fusion), slice={[256:7936], [0:1024]} | slice | bytes 62914560 | tf_op jit(solution)/shard_map/slice | solution.py:73
  818.8 31.3 %copy.15 = f32[7680,1024]{1,0:T(8,128)} copy(f32[7680,1024]{0,1:T(8,128)} %slice.99) | data formatting | bytes 62914560 | tf_op jit(solution)/shard_map/slice | solution.py:73
  850.3 57.9 %fusion.10 = f32[15,1024,512]{1,2,0:T(8,128)} fusion(f32[15,512,1024]{2,1,0:T(8,128)} %bitcast.39, f32[16,512,512]{2,1,0:T(8,128)} %all-gather.5.cloned.1.call-done), kind=kOutput, calls=%fused_computation.14 | convolution fusion | flops 48318382080 | bytes 78643200 | tf_op jit(solution)/shard_map/kij,kin->kjn/dot_general | solution.py:74
  908.2 23.0 %slice.96 = f32[8192,1024]{0,1:T(8,128)} slice(f32[8448,1024]{0,1:T(8,128)} %pad_maximum_fusion), slice={[0:8192], [0:1024]} | slice | bytes 67108864 | tf_op jit(solution)/shard_map/slice | solution.py:107
  932.5 3.8 fusion.20
  936.3 7.5 copy-done
  944.1 3.3 fusion.19
  947.4 21.8 %pad_maximum_fusion.1 = f32[8192,1024]{1,0:T(8,128)} fusion(f32[256,1024]{1,0:T(8,128)S(1)} %fusion.20, f32[7680,1024]{1,0:T(8,128)} %bitcast.38, f32[256,1024]{1,0:T(8,128)S(1)} %fusion.19), kind=kLoop, calls=%fused_computation.5 | loop fusion | flops 16777216 | bytes 67108864 | tf_op jit(solution)/shard_map/concatenate | solution.py:77
  (31 shorter events, 10.6 us)
Async XLA Ops:
  7.2 132.0 %all-gather.3.cloned.1.call-start = ((), (), s32[]{:S(2)}) async-start(), calls=%async_computation | async-start | bytes 17825792 | tf_op jit(solution)/shard_map/all_gather | solution.py:89
  7.9 258.1 %all-gather.5.cloned.1.call-start = ((), (), s32[]{:S(2)}) async-start(), calls=%async_computation.1 | async-start | bytes 17825792 | tf_op jit(solution)/shard_map/all_gather | solution.py:98
  8.6 393.3 %all-reduce.3.cloned.1.call-start = ((), (), s32[]{:S(2)}) async-start(), calls=%async_computation.2 | async-start | bytes 8388608 | tf_op jit(solution)/shard_map/psum | solution.py:9
  517.1 18.1 %copy-start.2 = (f32[2,512,512]{2,1,0:T(8,128)S(1)}, f32[2,512,512]{2,1,0:T(8,128)}, u32[]{:S(2)}) copy-start(f32[2,512,512]{2,1,0:T(8,128)} %get-tuple-element.7) | copy-start | bytes 6291460
  529.3 200.8 %collective-permute-start.1 = (f32[8448,256]{0,1:T(8,128)}, f32[8448,256]{0,1:T(8,128)}, u32[]{:S(2)}, u32[]{:S(2)}) collective-permute-start(f32[8448,256]{0,1:T(8,128)} %get-tuple-element.12), channel_id=1, source_target_pairs={{1,0},{2,1},{3,2},{4,3},{5,4},{6,5},{7,6},{8,7},{9,8},{10,9},{11,1... | collective-permute-start | bytes 25952264 | tf_op jit(solution)/shard_map/ppermute | solution.py:27
  529.7 220.8 %collective-permute-start = (f32[8448,256]{0,1:T(8,128)}, f32[8448,256]{0,1:T(8,128)}, u32[]{:S(2)}, u32[]{:S(2)}) collective-permute-start(f32[8448,256]{0,1:T(8,128)} %get-tuple-element.11), channel_id=1, source_target_pairs={{0,1},{1,2},{2,3},{3,4},{4,5},{5,6},{6,7},{7,8},{8,9},{9,10},{10,1... | collective-permute-start | bytes 25952264 | tf_op jit(solution)/shard_map/ppermute | solution.py:24
  533.9 398.6 %collective-permute-start.5 = (f32[1,512,512]{2,1,0:T(8,128)}, f32[1,512,512]{2,1,0:T(8,128)}, u32[]{:S(2)}, u32[]{:S(2)}) collective-permute-start(f32[1,512,512]{2,1,0:T(8,128)} %get-tuple-element.14), channel_id=1, source_target_pairs={{16,0},{0,16},{17,1},{1,17},{18,2},{2,18},{19,3},{3,19},{20,4},{4,... | collective-permute-start | bytes 3145736 | tf_op jit(solution)/shard_map/ppermute | solution.py:15
  535.3 193.8 %collective-permute-start.2 = (f32[1,512,512]{2,1,0:T(8,128)S(1)}, f32[1,512,512]{2,1,0:T(8,128)S(1)}, u32[]{:S(2)}, u32[]{:S(2)}) collective-permute-start(f32[1,512,512]{2,1,0:T(8,128)S(1)} %get-tuple-element.16), channel_id=1, source_target_pairs={{1,0},{2,1},{3,2},{4,3},{5,4},{6,5},{7,6},{8,7},{9,8},{10,9},{11,1... | collective-permute-start | bytes 3145736 | tf_op jit(solution)/shard_map/ppermute | solution.py:15
  570.0 201.1 %copy-start.1 = (f32[8448,512]{0,1:T(8,128)}, f32[8448,512]{0,1:T(8,128)S(1)}, u32[]{:S(2)}) copy-start(f32[8448,512]{0,1:T(8,128)S(1)} %fusion.12) | copy-start | bytes 51904516
  729.1 1.0 copy-start.4
  795.9 136.6 %collective-permute-start.4 = (f32[256,1024]{0,1:T(8,128)S(1)}, f32[256,1024]{0,1:T(8,128)}, u32[]{:S(2)}, u32[]{:S(2)}) collective-permute-start(f32[256,1024]{0,1:T(8,128)S(1)} %get-tuple-element.9), channel_id=1, source_target_pairs={{16,0},{0,16},{17,1},{1,17},{18,2},{2,18},{19,3},{3,19},{20,4},{4,... | collective-permute-start | bytes 3145736 | tf_op jit(solution)/shard_map/ppermute | solution.py:27
  850.1 86.3 %collective-permute-start.3 = (f32[256,1024]{0,1:T(8,128)S(1)}, f32[256,1024]{0,1:T(8,128)}, u32[]{:S(2)}, u32[]{:S(2)}) collective-permute-start(f32[256,1024]{0,1:T(8,128)S(1)} %get-tuple-element.10), channel_id=1, source_target_pairs={{0,16},{16,0},{1,17},{17,1},{2,18},{18,2},{3,19},{19,3},{4,20},{20... | collective-permute-start | bytes 3145736 | tf_op jit(solution)/shard_map/ppermute | solution.py:24
  932.5 11.3 %copy-start = (f32[8192,1024]{0,1:T(8,128)S(1)}, f32[8192,1024]{0,1:T(8,128)}, u32[]{:S(2)}) copy-start(f32[8192,1024]{0,1:T(8,128)} %slice.96) | copy-start | bytes 100663296
  932.5 11.6 %copy-start.3 = (f32[512,512]{1,0:T(8,128)S(1)}, f32[512,512]{1,0:T(8,128)}, u32[]{:S(2)}) copy-start(f32[512,512]{1,0:T(8,128)} %get-tuple-element.13) | copy-start | bytes 3145732
Sparse Core Ops, SparseCore 0:
  10.2 128.9 all-gather.2
  141.3 124.6 all-gather.4
  269.2 105.5 all-reduce.2
where the time goes:
time: 986 us; the launch traced here: 976 us
  waiting for transfers between devices  415 us (42%)
  matrix products  316 us (32%)
  local copies, waits for them, and re-layouts  173 us (18%)
  other arithmetic  52.9 us (5%)
  between operations  14.1 us (1%)
    ppermute x2, waiting for transfers between devices, passed_along(): return lax.ppermute(block, axis, route)  159 us
    all_gather x1, waiting for transfers between devices, per_device(): first_full = lax.all_gather(accum_first, 'col', axis=1, tiled=True)  130 us
    all_gather x1, waiting for transfers between devices, per_device(): second_full = lax.all_gather(accum_second, 'col', axis=1, tiled=True)  124 us
    dot_general x1, matrix products, aligned_right(): jnp.einsum('nki,kij->nkj', shaped, blocks, precision=lax.Precision.HIGHEST)  115 us
    concatenate x3, local copies, waits for them, and re-layouts, per_device(): stacked = jnp.concatenate([turned_rows, schur_rows], axis=0)  70.6 us
    dot_general x1, matrix products, per_device(): jnp.einsum('kij,kin->kjn', first_full, shaped, precision=lax.Precision.HI...  60.6 us
    dot_general x1, matrix products, straddle_left(): jnp.einsum('kij,kin->kjn', blocks[1:count], inner, precision=lax.Precisio...  57.9 us
    slice x2, local copies, waits for them, and re-layouts, straddle_left(): inner = extended[width:count * width].reshape(count - 1, width, cols)  53 us
  transfers between devices with their start and end apart: 9, of which 3 were waited for; matrix products, arithmetic and copies ran while one was open for 39% of the time, Pallas kernels for 0%

commit v1 on v0

--- a/solution.py
+++ b/solution.py
@@ -95,7 +95,12 @@
     first_cols = spread(chosen, "row", owner_row)
     stacked = jnp.concatenate([turned_rows, schur_rows], axis=0)
     turned = aligned_right(stacked, first_cols)
-    second_full = lax.all_gather(accum_second, "col", axis=1, tiled=True)
+    ring = [accum_second]
+    for hop in range(15):
+        ring.append(lax.ppermute(ring[-1], "col", [(dev, (dev + 1) % 16) for dev in range(16)]))
+    second_full = jnp.roll(
+        jnp.concatenate(ring[::-1], axis=1), (lax.axis_index("col") + 1) * ring[0].shape[1], axis=1
+    )
     chosen_second = lax.dynamic_slice_in_dim(second_full, owner_offset, per_col, 0)
     second_cols = spread(chosen_second, "row", owner_row)
     next_col = passed_along(second_cols[0:1], "col", -1)

time: 986 us -> 1250 us (1.27)
  matrix products: 316 us -> 482 us
  local copies, waits for them, and re-layouts: 173 us -> 229 us
  starting transfers between devices: 4.62 us -> 31.9 us
  waiting for transfers between devices: 415 us -> 428 us
    ppermute x0 -> x15, waiting for transfers between devices: none -> 307 us  [per_device(): lax.ppermute(ring[-1], 'col', [(dev, (dev + 1) % 16) for dev in range(16)])]
    dot_general x1, matrix products: 57.9 us -> 221 us  [straddle_left(): jnp.einsum('kij,kin->kjn', blocks[1:count], inner, precision=lax.Precisio...]
    ppermute x2, waiting for transfers between devices: 159 us -> 0.01 us  [passed_along(): return lax.ppermute(block, axis, route)]
    all_gather x1, waiting for transfers between devices: 130 us -> 0.01 us  [per_device(): first_full = lax.all_gather(accum_first, 'col', axis=1, tiled=True)]
    all_gather x1 -> x0, waiting for transfers between devices: 124 us -> none  [per_device(): second_full = lax.all_gather(accum_second, 'col', axis=1, tiled=True)]
    ppermute x2, waiting for transfers between devices: 0.01 us -> 121 us  [padded(): lax.ppermute(lax.slice_in_dim(block, block.shape[dim] - width, None, axis...]
    unnamed x12 -> x91, local copies, waits for them, and re-layouts: 11.6 us -> 53.3 us
    ppermute x2, starting transfers between devices: 1.66 us -> 16.2 us  [padded(): lax.ppermute(lax.slice_in_dim(block, 0, width, axis=dim), axis, backward)]
  transfers between devices with their start and end apart: 9 -> 23, of which waited for: 3 -> 16; matrix products, arithmetic and copies ran while one was open for 39% -> 47% of each run, Pallas kernels for 0% -> 0%
where the time goes in v1:
time: 1250 us; the launch traced here: 1240 us
  matrix products  482 us (39%)
  waiting for transfers between devices  428 us (34%)
  local copies, waits for them, and re-layouts  229 us (18%)
  other arithmetic  52.8 us (4%)
  starting transfers between devices  31.9 us (3%)
  between operations  15 us (1%)
    ppermute x15, waiting for transfers between devices, per_device(): lax.ppermute(ring[-1], 'col', [(dev, (dev + 1) % 16) for dev in range(16)])  307 us
    dot_general x1, matrix products, straddle_left(): jnp.einsum('kij,kin->kjn', blocks[1:count], inner, precision=lax.Precisio...  221 us
    ppermute x2, waiting for transfers between devices, padded(): lax.ppermute(lax.slice_in_dim(block, block.shape[dim] - width, None, axis...  121 us
    dot_general x1, matrix products, aligned_right(): jnp.einsum('nki,kij->nkj', shaped, blocks, precision=lax.Precision.HIGHEST)  115 us
    concatenate x3, local copies, waits for them, and re-layouts, per_device(): stacked = jnp.concatenate([turned_rows, schur_rows], axis=0)  70.9 us
    dot_general x1, matrix products, per_device(): jnp.einsum('kij,kin->kjn', first_full, shaped, precision=lax.Precision.HI...  60.1 us
    unnamed x91, local copies, waits for them, and re-layouts  53.3 us
    slice x2, local copies, waits for them, and re-layouts, straddle_left(): inner = extended[width:count * width].reshape(count - 1, width, cols)  52.6 us
  transfers between devices with their start and end apart: 23, of which 16 were waited for; matrix products, arithmetic and copies ran while one was open for 47% of the time, Pallas kernels for 0%

profile of v1, /device:TPU:1, one launch (start us, length us, event | category | flops | bytes accessed | tf_op | source)
XLA Modules:
  0.0 1239.2 jit_solution(16145435463312079897)
XLA Ops:
  27.2 17.8 %collective-permute-done.1 = f32[16,32,512]{2,1,0:T(8,128)S(1)} collective-permute-done((f32[16,32,512]{2,1,0:T(8,128)S(1)}, f32[16,32,512]{2,1,0:T(8,128)S(1)}, u32[]{:S(2)}, u32[]{:S(2)}) %collective-permute-start.1) | collective-permute-done | bytes 1048608 | tf_op jit(solution)/shard_map/ppermute | solution.py:100
  47.5 20.4 %collective-permute-done.2 = f32[16,32,512]{2,1,0:T(8,128)S(1)} collective-permute-done((f32[16,32,512]{2,1,0:T(8,128)S(1)}, f32[16,32,512]{2,1,0:T(8,128)S(1)}, u32[]{:S(2)}, u32[]{:S(2)}) %collective-permute-start.2) | collective-permute-done | bytes 1048608 | tf_op jit(solution)/shard_map/ppermute | solution.py:100
  69.0 24.1 %collective-permute-done.3 = f32[16,32,512]{2,1,0:T(8,128)S(1)} collective-permute-done((f32[16,32,512]{2,1,0:T(8,128)S(1)}, f32[16,32,512]{2,1,0:T(8,128)S(1)}, u32[]{:S(2)}, u32[]{:S(2)}) %collective-permute-start.3) | collective-permute-done | bytes 1048608 | tf_op jit(solution)/shard_map/ppermute | solution.py:100
  95.6 37.9 %collective-permute-done.4 = f32[16,32,512]{2,1,0:T(8,128)S(1)} collective-permute-done((f32[16,32,512]{2,1,0:T(8,128)S(1)}, f32[16,32,512]{2,1,0:T(8,128)S(1)}, u32[]{:S(2)}, u32[]{:S(2)}) %collective-permute-start.4) | collective-permute-done | bytes 1048608 | tf_op jit(solution)/shard_map/ppermute | solution.py:100
  134.6 39.5 %collective-permute-done.5 = f32[16,32,512]{2,1,0:T(8,128)S(1)} collective-permute-done((f32[16,32,512]{2,1,0:T(8,128)S(1)}, f32[16,32,512]{2,1,0:T(8,128)S(1)}, u32[]{:S(2)}, u32[]{:S(2)}) %collective-permute-start.5) | collective-permute-done | bytes 1048608 | tf_op jit(solution)/shard_map/ppermute | solution.py:100
  175.1 16.9 %collective-permute-done.6 = f32[16,32,512]{2,1,0:T(8,128)S(1)} collective-permute-done((f32[16,32,512]{2,1,0:T(8,128)S(1)}, f32[16,32,512]{2,1,0:T(8,128)S(1)}, u32[]{:S(2)}, u32[]{:S(2)}) %collective-permute-start.6) | collective-permute-done | bytes 1048608 | tf_op jit(solution)/shard_map/ppermute | solution.py:100
  193.0 16.9 %collective-permute-done.7 = f32[16,32,512]{2,1,0:T(8,128)S(1)} collective-permute-done((f32[16,32,512]{2,1,0:T(8,128)S(1)}, f32[16,32,512]{2,1,0:T(8,128)S(1)}, u32[]{:S(2)}, u32[]{:S(2)}) %collective-permute-start.7) | collective-permute-done | bytes 1048608 | tf_op jit(solution)/shard_map/ppermute | solution.py:100
  210.9 16.9 %collective-permute-done.8 = f32[16,32,512]{2,1,0:T(8,128)S(1)} collective-permute-done((f32[16,32,512]{2,1,0:T(8,128)S(1)}, f32[16,32,512]{2,1,0:T(8,128)S(1)}, u32[]{:S(2)}, u32[]{:S(2)}) %collective-permute-start.8) | collective-permute-done | bytes 1048608 | tf_op jit(solution)/shard_map/ppermute | solution.py:100
  300.4 17.0 %collective-permute-done.13 = f32[16,32,512]{2,1,0:T(8,128)} collective-permute-done((f32[16,32,512]{2,1,0:T(8,128)S(1)}, f32[16,32,512]{2,1,0:T(8,128)}, u32[]{:S(2)}, u32[]{:S(2)}) %collective-permute-start.13) | collective-permute-done | bytes 1048608 | tf_op jit(solution)/shard_map/ppermute | solution.py:100
  317.6 17.1 %collective-permute-done.14 = f32[16,32,512]{2,1,0:T(8,128)} collective-permute-done((f32[16,32,512]{2,1,0:T(8,128)}, f32[16,32,512]{2,1,0:T(8,128)}, u32[]{:S(2)}, u32[]{:S(2)}) %collective-permute-start.14) | collective-permute-done | bytes 1048608 | tf_op jit(solution)/shard_map/ppermute | solution.py:100
  375.4 60.1 %fusion.30 = f32[16,512,1024]{2,1,0:T(8,128)} fusion(f32[16,512,512]{2,1,0:T(8,128)} %all-gather.2.cloned.1.call-done, f32[16,512,1024]{2,1,0:T(8,128)} %bitcast.33), kind=kOutput, calls=%fused_computation.74 | convolution fusion | flops 51539607552 | bytes 83886080 | tf_op jit(solution)/shard_map/kij,kin->kjn/dot_general | solution.py:91
  435.5 43.0 %concatenate.35 = f32[8192,2,512]{2,1,0:T(2,128)} reshape(f32[16,512,1024]{2,1,0:T(8,128)} %fusion.30) | data formatting | bytes 67108864 | tf_op jit(solution)/shard_map/concatenate | solution.py:96
  478.5 27.6 %copy.12 = f32[8192,2,512]{2,0,1:T(8,128)} copy(f32[8192,2,512]{2,1,0:T(2,128)} %concatenate.35) | data formatting | bytes 67108864 | tf_op jit(solution)/shard_map/concatenate | solution.py:96
  506.1 115.2 %fusion = f32[2,512,8448]{2,1,0:T(8,128)} fusion(f32[2,512,512]{2,1,0:T(8,128)} %get-tuple-element.6, f32[256,2,512]{2,0,1:T(8,128)S(1)} %copy.13, f32[8192,2,512]{2,0,1:T(8,128)} %copy.12), kind=kOutput, calls=%fused_computation | convolution fusion | flops 53158871040 | bytes 71303168 | tf_op jit(solution)/shard_map/nki,kij->nkj/dot_general | solution.py:40
  671.3 34.6 %fusion.12 = f32[8448,512]{0,1:T(8,128)S(1)} fusion(f32[8448,1024]{0,1:T(8,128)} %bitcast.30, f32[2,512,512]{2,1,0:T(8,128)S(1)} %copy-done.3), kind=kOutput, calls=%fused_computation.16 | convolution fusion | flops 26575110144 | bytes 35651584 | tf_op jit(solution)/shard_map/nki,kij->nkj/dot_general | solution.py:53
  705.9 120.8 %collective-permute-done.15 = f32[8448,256]{0,1:T(8,128)} collective-permute-done((f32[8448,256]{0,1:T(8,128)}, f32[8448,256]{0,1:T(8,128)}, u32[]{:S(2)}, u32[]{:S(2)}) %collective-permute-start.15) | collective-permute-done | bytes 8650784 | tf_op jit(solution)/shard_map/ppermute | solution.py:24
  826.7 20.4 %fusion.8 = f32[8448,256]{0,1:T(8,128)} fusion(f32[8448,1024]{0,1:T(8,128)} %bitcast.31, f32[8448,256]{0,1:T(8,128)} %collective-permute-done.15, f32[512,512]{1,0:T(8,128)S(1)} %get-tuple-element.13), kind=kOutput, calls=%fused_computation.12 | convolution fusion | flops 13291880448 | bytes 52428800 | tf_op jit(solution)/shard_map/dot_general | solution.py:33
  847.2 20.5 %fusion.4 = f32[8448,256]{0,1:T(8,128)} fusion(f32[8448,256]{0,1:T(8,128)} %collective-permute-done.16, f32[8448,1024]{0,1:T(8,128)} %bitcast.32, f32[512,512]{1,0:T(8,128)S(1)} %bitcast.37), kind=kOutput, calls=%fused_computation.7 | convolution fusion | flops 13291880448 | bytes 52428800 | tf_op jit(solution)/shard_map/dot_general | solution.py:33
  870.7 23.1 %pad_maximum_fusion = f32[8448,1024]{0,1:T(8,128)} fusion(f32[8448,256]{0,1:T(8,128)} %fusion.4, f32[8448,512]{0,1:T(8,128)} %copy-done.1, f32[8448,256]{0,1:T(8,128)} %fusion.8), kind=kLoop, calls=%fused_computation.4 | loop fusion | flops 17301504 | bytes 69206016 | tf_op jit(solution)/shard_map/concatenate | solution.py:56
  895.3 21.7 %slice.98 = f32[7680,1024]{0,1:T(8,128)} slice(f32[8448,1024]{0,1:T(8,128)} %pad_maximum_fusion), slice={[256:7936], [0:1024]} | slice | bytes 62914560 | tf_op jit(solution)/shard_map/slice | solution.py:73
  917.0 30.9 %copy.15 = f32[7680,1024]{1,0:T(8,128)} copy(f32[7680,1024]{0,1:T(8,128)} %slice.98) | data formatting | bytes 62914560 | tf_op jit(solution)/shard_map/slice | solution.py:73
  947.9 221.4 %fusion.10 = f32[15,512,1024]{2,1,0:T(8,128)} fusion(f32[15,512,1024]{2,1,0:T(8,128)} %bitcast.35, f32[16,512,512]{2,1,0:T(8,128)} %fusion.42), kind=kOutput, calls=%fused_computation.14 | convolution fusion | flops 48318382080 | bytes 79691776 | tf_op jit(solution)/shard_map/kij,kin->kjn/dot_general | solution.py:74
  1169.3 23.4 %slice.97 = f32[8192,1024]{0,1:T(8,128)} slice(f32[8448,1024]{0,1:T(8,128)} %pad_maximum_fusion), slice={[0:8192], [0:1024]} | slice | bytes 67108864 | tf_op jit(solution)/shard_map/slice | solution.py:112
  1210.1 21.8 %pad_maximum_fusion.1 = f32[8192,1024]{1,0:T(8,128)} fusion(f32[256,1024]{1,0:T(8,128)S(1)} %fusion.15, f32[7680,1024]{1,0:T(8,128)} %bitcast.34, f32[256,1024]{1,0:T(8,128)S(1)} %fusion.17), kind=kLoop, calls=%fused_computation.5 | loop fusion | flops 16777216 | bytes 67108864 | tf_op jit(solution)/shard_map/concatenate | solution.py:77
  (140 shorter events, 214.8 us)
Async XLA Ops:
  7.2 350.4 %copy-start.5 = (f32[16,32,512]{2,1,0:T(8,128)S(1)}, f32[16,32,512]{2,1,0:T(8,128)}, u32[]{:S(2)}) copy-start(f32[16,32,512]{2,1,0:T(8,128)} %param.7) | copy-start | bytes 3145732
  7.2 363.1 %all-gather.2.cloned.1.call-start = ((), (), s32[]{:S(2)}) async-start(), calls=%async_computation | async-start | bytes 17825792 | tf_op jit(solution)/shard_map/all_gather | solution.py:89
  7.9 498.2 %all-reduce.3.cloned.1.call-start = ((), (), s32[]{:S(2)}) async-start(), calls=%async_computation.1 | async-start | bytes 8388608 | tf_op jit(solution)/shard_map/psum | solution.py:9
  8.0 16.9 %collective-permute-start = (f32[16,32,512]{2,1,0:T(8,128)}, f32[16,32,512]{2,1,0:T(8,128)S(1)}, u32[]{:S(2)}, u32[]{:S(2)}) collective-permute-start(f32[16,32,512]{2,1,0:T(8,128)} %param.7), channel_id=1, source_target_pairs={{0,1},{1,2},{2,3},{3,4},{4,5},{5,6},{6,7},{7,8},{8,9},{9,10},{10,1... | collective-permute-start | bytes 3145736 | tf_op jit(solution)/shard_map/ppermute | solution.py:100
  24.8 20.2 %collective-permute-start.1 = (f32[16,32,512]{2,1,0:T(8,128)S(1)}, f32[16,32,512]{2,1,0:T(8,128)S(1)}, u32[]{:S(2)}, u32[]{:S(2)}) collective-permute-start(f32[16,32,512]{2,1,0:T(8,128)S(1)} %collective-permute-done), channel_id=1, source_target_pairs={{0,1},{1,2},{2,3},{3,4},{4,5},{5,6},{6,7},{7,8},{8,9},{9,10},{10,1... | collective-permute-start | bytes 3145736 | tf_op jit(solution)/shard_map/ppermute | solution.py:100
  45.0 22.9 %collective-permute-start.2 = (f32[16,32,512]{2,1,0:T(8,128)S(1)}, f32[16,32,512]{2,1,0:T(8,128)S(1)}, u32[]{:S(2)}, u32[]{:S(2)}) collective-permute-start(f32[16,32,512]{2,1,0:T(8,128)S(1)} %collective-permute-done.1), channel_id=1, source_target_pairs={{0,1},{1,2},{2,3},{3,4},{4,5},{5,6},{6,7},{7,8},{8,9},{9,10},{10,1... | collective-permute-start | bytes 3145736 | tf_op jit(solution)/shard_map/ppermute | solution.py:100
  69.0 24.1 %collective-permute-start.3 = (f32[16,32,512]{2,1,0:T(8,128)S(1)}, f32[16,32,512]{2,1,0:T(8,128)S(1)}, u32[]{:S(2)}, u32[]{:S(2)}) collective-permute-start(f32[16,32,512]{2,1,0:T(8,128)S(1)} %collective-permute-done.2), channel_id=1, source_target_pairs={{0,1},{1,2},{2,3},{3,4},{4,5},{5,6},{6,7},{7,8},{8,9},{9,10},{10,1... | collective-permute-start | bytes 3145736 | tf_op jit(solution)/shard_map/ppermute | solution.py:100
  94.1 39.5 %collective-permute-start.4 = (f32[16,32,512]{2,1,0:T(8,128)S(1)}, f32[16,32,512]{2,1,0:T(8,128)S(1)}, u32[]{:S(2)}, u32[]{:S(2)}) collective-permute-start(f32[16,32,512]{2,1,0:T(8,128)S(1)} %collective-permute-done.3), channel_id=1, source_target_pairs={{0,1},{1,2},{2,3},{3,4},{4,5},{5,6},{6,7},{7,8},{8,9},{9,10},{10,1... | collective-permute-start | bytes 3145736 | tf_op jit(solution)/shard_map/ppermute | solution.py:100
  134.6 39.5 %collective-permute-start.5 = (f32[16,32,512]{2,1,0:T(8,128)S(1)}, f32[16,32,512]{2,1,0:T(8,128)S(1)}, u32[]{:S(2)}, u32[]{:S(2)}) collective-permute-start(f32[16,32,512]{2,1,0:T(8,128)S(1)} %collective-permute-done.4), channel_id=1, source_target_pairs={{0,1},{1,2},{2,3},{3,4},{4,5},{5,6},{6,7},{7,8},{8,9},{9,10},{10,1... | collective-permute-start | bytes 3145736 | tf_op jit(solution)/shard_map/ppermute | solution.py:100
  175.1 16.9 %collective-permute-start.6 = (f32[16,32,512]{2,1,0:T(8,128)S(1)}, f32[16,32,512]{2,1,0:T(8,128)S(1)}, u32[]{:S(2)}, u32[]{:S(2)}) collective-permute-start(f32[16,32,512]{2,1,0:T(8,128)S(1)} %collective-permute-done.5), channel_id=1, source_target_pairs={{0,1},{1,2},{2,3},{3,4},{4,5},{5,6},{6,7},{7,8},{8,9},{9,10},{10,1... | collective-permute-start | bytes 3145736 | tf_op jit(solution)/shard_map/ppermute | solution.py:100
  193.0 16.9 %collective-permute-start.7 = (f32[16,32,512]{2,1,0:T(8,128)S(1)}, f32[16,32,512]{2,1,0:T(8,128)S(1)}, u32[]{:S(2)}, u32[]{:S(2)}) collective-permute-start(f32[16,32,512]{2,1,0:T(8,128)S(1)} %collective-permute-done.6), channel_id=1, source_target_pairs={{0,1},{1,2},{2,3},{3,4},{4,5},{5,6},{6,7},{7,8},{8,9},{9,10},{10,1... | collective-permute-start | bytes 3145736 | tf_op jit(solution)/shard_map/ppermute | solution.py:100
  210.9 16.9 %collective-permute-start.8 = (f32[16,32,512]{2,1,0:T(8,128)S(1)}, f32[16,32,512]{2,1,0:T(8,128)S(1)}, u32[]{:S(2)}, u32[]{:S(2)}) collective-permute-start(f32[16,32,512]{2,1,0:T(8,128)S(1)} %collective-permute-done.7), channel_id=1, source_target_pairs={{0,1},{1,2},{2,3},{3,4},{4,5},{5,6},{6,7},{7,8},{8,9},{9,10},{10,1... | collective-permute-start | bytes 3145736 | tf_op jit(solution)/shard_map/ppermute | solution.py:100
  228.8 16.9 %collective-permute-start.9 = (f32[16,32,512]{2,1,0:T(8,128)S(1)}, f32[16,32,512]{2,1,0:T(8,128)S(1)}, u32[]{:S(2)}, u32[]{:S(2)}) collective-permute-start(f32[16,32,512]{2,1,0:T(8,128)S(1)} %collective-permute-done.8), channel_id=1, source_target_pairs={{0,1},{1,2},{2,3},{3,4},{4,5},{5,6},{6,7},{7,8},{8,9},{9,10},{10,1... | collective-permute-start | bytes 3145736 | tf_op jit(solution)/shard_map/ppermute | solution.py:100
  246.8 16.9 %collective-permute-start.10 = (f32[16,32,512]{2,1,0:T(8,128)S(1)}, f32[16,32,512]{2,1,0:T(8,128)S(1)}, u32[]{:S(2)}, u32[]{:S(2)}) collective-permute-start(f32[16,32,512]{2,1,0:T(8,128)S(1)} %collective-permute-done.9), channel_id=1, source_target_pairs={{0,1},{1,2},{2,3},{3,4},{4,5},{5,6},{6,7},{7,8},{8,9},{9,10},{10,1... | collective-permute-start | bytes 3145736 | tf_op jit(solution)/shard_map/ppermute | solution.py:100
  264.6 16.9 %collective-permute-start.11 = (f32[16,32,512]{2,1,0:T(8,128)S(1)}, f32[16,32,512]{2,1,0:T(8,128)S(1)}, u32[]{:S(2)}, u32[]{:S(2)}) collective-permute-start(f32[16,32,512]{2,1,0:T(8,128)S(1)} %collective-permute-done.10), channel_id=1, source_target_pairs={{0,1},{1,2},{2,3},{3,4},{4,5},{5,6},{6,7},{7,8},{8,9},{9,10},{10,1... | collective-permute-start | bytes 3145736 | tf_op jit(solution)/shard_map/ppermute | solution.py:100
  282.5 16.9 %collective-permute-start.12 = (f32[16,32,512]{2,1,0:T(8,128)S(1)}, f32[16,32,512]{2,1,0:T(8,128)S(1)}, u32[]{:S(2)}, u32[]{:S(2)}) collective-permute-start(f32[16,32,512]{2,1,0:T(8,128)S(1)} %collective-permute-done.11), channel_id=1, source_target_pairs={{0,1},{1,2},{2,3},{3,4},{4,5},{5,6},{6,7},{7,8},{8,9},{9,10},{10,1... | collective-permute-start | bytes 3145736 | tf_op jit(solution)/shard_map/ppermute | solution.py:100
  300.4 17.1 %collective-permute-start.13 = (f32[16,32,512]{2,1,0:T(8,128)S(1)}, f32[16,32,512]{2,1,0:T(8,128)}, u32[]{:S(2)}, u32[]{:S(2)}) collective-permute-start(f32[16,32,512]{2,1,0:T(8,128)S(1)} %collective-permute-done.12), channel_id=1, source_target_pairs={{0,1},{1,2},{2,3},{3,4},{4,5},{5,6},{6,7},{7,8},{8,9},{9,10},{10,1... | collective-permute-start | bytes 3145736 | tf_op jit(solution)/shard_map/ppermute | solution.py:100
  317.5 17.2 %collective-permute-start.14 = (f32[16,32,512]{2,1,0:T(8,128)}, f32[16,32,512]{2,1,0:T(8,128)}, u32[]{:S(2)}, u32[]{:S(2)}) collective-permute-start(f32[16,32,512]{2,1,0:T(8,128)} %collective-permute-done.13), channel_id=1, source_target_pairs={{0,1},{1,2},{2,3},{3,4},{4,5},{5,6},{6,7},{7,8},{8,9},{9,10},{10,1... | collective-permute-start | bytes 3145736 | tf_op jit(solution)/shard_map/ppermute | solution.py:100
  633.5 193.3 %collective-permute-start.15 = (f32[8448,256]{0,1:T(8,128)}, f32[8448,256]{0,1:T(8,128)}, u32[]{:S(2)}, u32[]{:S(2)}) collective-permute-start(f32[8448,256]{0,1:T(8,128)} %get-tuple-element.11), channel_id=1, source_target_pairs={{0,1},{1,2},{2,3},{3,4},{4,5},{5,6},{6,7},{7,8},{8,9},{9,10},{10,1... | collective-permute-start | bytes 25952264 | tf_op jit(solution)/shard_map/ppermute | solution.py:24
  633.5 213.7 %collective-permute-start.16 = (f32[8448,256]{0,1:T(8,128)}, f32[8448,256]{0,1:T(8,128)}, u32[]{:S(2)}, u32[]{:S(2)}) collective-permute-start(f32[8448,256]{0,1:T(8,128)} %get-tuple-element.12), channel_id=1, source_target_pairs={{1,0},{2,1},{3,2},{4,3},{5,4},{6,5},{7,6},{8,7},{9,8},{10,9},{11,1... | collective-permute-start | bytes 25952264 | tf_op jit(solution)/shard_map/ppermute | solution.py:27
  650.7 548.5 %collective-permute-start.19 = (f32[1,512,512]{2,1,0:T(8,128)}, f32[1,512,512]{2,1,0:T(8,128)}, u32[]{:S(2)}, u32[]{:S(2)}) collective-permute-start(f32[1,512,512]{2,1,0:T(8,128)} %constant_dynamic-slice_fusion), channel_id=1, source_target_pairs={{16,0},{0,16},{17,1},{1,17},{18,2},{2,18},{19,3},{3,19},{20,4},{4,... | collective-permute-start | bytes 3145736 | tf_op jit(solution)/shard_map/ppermute | solution.py:15
  666.5 180.7 %collective-permute-start.17 = (f32[1,512,512]{2,1,0:T(8,128)S(1)}, f32[1,512,512]{2,1,0:T(8,128)S(1)}, u32[]{:S(2)}, u32[]{:S(2)}) collective-permute-start(f32[1,512,512]{2,1,0:T(8,128)S(1)} %get-tuple-element.14), channel_id=1, source_target_pairs={{1,0},{2,1},{3,2},{4,3},{5,4},{6,5},{7,6},{8,7},{9,8},{10,9},{11,1... | collective-permute-start | bytes 3145736 | tf_op jit(solution)/shard_map/ppermute | solution.py:15
  893.9 305.4 %collective-permute-start.20 = (f32[256,1024]{0,1:T(8,128)}, f32[256,1024]{0,1:T(8,128)}, u32[]{:S(2)}, u32[]{:S(2)}) collective-permute-start(f32[256,1024]{0,1:T(8,128)} %get-tuple-element.9), channel_id=1, source_target_pairs={{16,0},{0,16},{17,1},{1,17},{18,2},{2,18},{19,3},{3,19},{20,4},{4,... | collective-permute-start | bytes 3145736 | tf_op jit(solution)/shard_map/ppermute | solution.py:27
  895.1 298.9 %collective-permute-start.18 = (f32[256,1024]{0,1:T(8,128)}, f32[256,1024]{0,1:T(8,128)}, u32[]{:S(2)}, u32[]{:S(2)}) collective-permute-start(f32[256,1024]{0,1:T(8,128)} %get-tuple-element.10), channel_id=1, source_target_pairs={{0,16},{16,0},{1,17},{17,1},{2,18},{18,2},{3,19},{19,3},{4,20},{20... | collective-permute-start | bytes 3145736 | tf_op jit(solution)/shard_map/ppermute | solution.py:24
  (28 other events, 719.0 us)
Sparse Core Ops, SparseCore 0:
  10.2 154.8 all-gather.1
  373.6 119.1 all-reduce.2
